TPU v7x, 256 devices: a whole 4x4x8 slice. The times are simulated.
256 devices in a mesh: layer: 16 (over z, core), dp: 16 (over x, y).
Axes of the slice: x: 4, y: 4, z: 8, core: 2. Of those that a mesh axis runs over, the one named last changes fastest.
Arguments:
- starts: float32 [16, 16, 32, 32, 128], P('layer', 'dp'), may hold values from -6 to 6
- weights: bfloat16 [64, 9, 128, 128], P('layer'), may hold values from -0.1875 to 0.1875
- biases: bfloat16 [64, 128], P('layer'), may hold values from -3 to 3
- adj_ends: float32 [16, 16, 32, 32, 128], P('layer', 'dp'), may hold values from -6 to 6
Outputs:
- block_ends: float32 [16, 16, 32, 32, 128], P('layer', 'dp')
- adjoint_starts: float32 [16, 16, 32, 32, 128], P('layer', 'dp')
- weight_grad: float32 [64, 9, 128, 128], P('layer')
- bias_grad: float32 [64, 128], P('layer')
All inputs are finite; a program needn't handle non-finite values.
Results may differ from a plain program's by a relative error of at most 0.039.
Values may be sent and summed in bfloat16 or wider, within the bound.
No kernel may reach another device: no remote copies, remote signals or barrier semaphores. Data moves between devices by JAX's collectives and lax.ppermute only.
A program may use at most 64 MiB of HBM per device.

v0:
```python
import math
import jax
import jax.numpy as jnp
from jax import lax
from jax.sharding import PartitionSpec as P

step_size = 0.25


def passed_along(x, axis, by):
    peers = lax.axis_size(axis)
    pairs = [(i, i + by) for i in range(peers) if 0 <= i + by < peers]
    return lax.ppermute(x, axis, pairs)


def convolve(rounded, kernel):
    count, map_side, _, channels = rounded.shape
    padded = jnp.pad(rounded, ((0, 0), (1, 1), (1, 1), (0, 0)))
    running = jnp.zeros((count * map_side * map_side, kernel.shape[2]), jnp.float32)
    for tap_index in range(9):
        row_off = tap_index // 3
        col_off = tap_index % 3
        view = padded[:, row_off : row_off + map_side, col_off : col_off + map_side, :].reshape(
            count * map_side * map_side, channels
        )
        running = running + jnp.dot(view, kernel[tap_index], preferred_element_type=jnp.float32)
    return running.reshape(count, map_side, map_side, kernel.shape[2])


def transposed(signal, kernel):
    count, map_side, _, channels = signal.shape
    padded = jnp.pad(signal, ((0, 0), (1, 1), (1, 1), (0, 0)))
    running = jnp.zeros((count * map_side * map_side, kernel.shape[1]), jnp.float32)
    for tap_index in range(9):
        row_off = 2 - tap_index // 3
        col_off = 2 - tap_index % 3
        view = padded[:, row_off : row_off + map_side, col_off : col_off + map_side, :].reshape(
            count * map_side * map_side, channels
        )
        running = running + lax.dot_general(
            view, kernel[tap_index], (((1,), (1,)), ((), ())), preferred_element_type=jnp.float32
        )
    return running.reshape(count, map_side, map_side, kernel.shape[1])


def correlate(rounded, signal):
    count, map_side, _, channels = rounded.shape
    padded = jnp.pad(rounded, ((0, 0), (1, 1), (1, 1), (0, 0)))
    flat_signal = signal.reshape(count * map_side * map_side, signal.shape[3])
    pieces = []
    for tap_index in range(9):
        row_off = tap_index // 3
        col_off = tap_index % 3
        view = padded[:, row_off : row_off + map_side, col_off : col_off + map_side, :].reshape(
            count * map_side * map_side, channels
        )
        pieces.append(
            lax.dot_general(
                view, flat_signal, (((0,), (0,)), ((), ())), preferred_element_type=jnp.float32
            )
        )
    return jnp.stack(pieces)


def activation_of(rounded, kernel, bias_row):
    return jnp.tanh(convolve(rounded, kernel) + bias_row.astype(jnp.float32))


def local(starts, weights, biases, adj_ends):
    layer_index = lax.axis_index("layer")
    blocks = lax.axis_size("layer")
    block_depth = weights.shape[0]
    coarse_step = block_depth * step_size
    map_side = starts.shape[2]
    image_total = starts.shape[1] * lax.axis_size("dp")
    grad_scale = 1.0 / (map_side * math.sqrt(image_total))
    first_state = starts[0]
    adjoint_guess = adj_ends[0]
    first_kernel = weights[0]
    first_bias = biases[0]

    def coarse_apply(current_state, kernel, bias_row):
        return current_state + coarse_step * activation_of(
            current_state.astype(jnp.bfloat16), kernel, bias_row
        )

    current_state = first_state
    for inner_pos in range(block_depth):
        current_state = current_state + step_size * activation_of(
            current_state.astype(jnp.bfloat16), weights[inner_pos], biases[inner_pos]
        )
    relaxed = current_state
    offset = relaxed - coarse_apply(first_state, first_kernel, first_bias)

    def advance(step_index, carried):
        produced = lax.cond(
            layer_index == step_index,
            lambda held: offset + coarse_apply(held, first_kernel, first_bias),
            lambda held: jnp.zeros_like(held),
            carried,
        )
        received = passed_along(produced, "layer", 1)
        return jnp.where(layer_index == step_index + 1, received, carried)

    entry = lax.fori_loop(0, blocks - 1, advance, first_state)
    saved_states = []
    saved_slopes = []
    current_state = entry
    for inner_pos in range(block_depth):
        rounded = current_state.astype(jnp.bfloat16)
        saved_states.append(rounded)
        activation = activation_of(rounded, weights[inner_pos], biases[inner_pos])
        saved_slopes.append(1.0 - activation * activation)
        current_state = current_state + step_size * activation
    adjoint = adjoint_guess
    for inner_pos in reversed(range(block_depth)):
        signal = (saved_slopes[inner_pos] * adjoint).astype(jnp.bfloat16)
        adjoint = adjoint + step_size * transposed(signal, weights[inner_pos])
    backed = adjoint

    def coarse_adjoint(difference):
        signal = (saved_slopes[0] * difference).astype(jnp.bfloat16)
        return difference + coarse_step * transposed(signal, first_kernel)

    def retreat(step_index, carried):
        sender = blocks - 1 - step_index
        produced = lax.cond(
            layer_index == sender,
            lambda held: backed + coarse_adjoint(held - adjoint_guess),
            lambda held: jnp.zeros_like(held),
            carried,
        )
        received = passed_along(produced.astype(jnp.bfloat16), "layer", -1).astype(produced.dtype)
        return jnp.where(layer_index == sender - 1, received, carried)

    exit_adjoint = lax.fori_loop(0, blocks - 1, retreat, adjoint_guess)
    kernel_grads = [None] * block_depth
    bias_grads = [None] * block_depth
    adjoint = exit_adjoint
    for inner_pos in reversed(range(block_depth)):
        signal = (saved_slopes[inner_pos] * adjoint).astype(jnp.bfloat16)
        kernel_part = correlate(saved_states[inner_pos], signal) * grad_scale
        bias_part = jnp.sum(signal.astype(jnp.float32), axis=(0, 1, 2)) * grad_scale
        kernel_grads[inner_pos] = kernel_part
        bias_grads[inner_pos] = bias_part
        adjoint = adjoint + step_size * transposed(signal, weights[inner_pos])
    kernel_stack = jnp.stack(kernel_grads)
    bias_stack = jnp.stack(bias_grads)
    kernel_stack, bias_stack = (
        lax.psum(kernel_stack.astype(jnp.bfloat16), "dp").astype(jnp.float32),
        lax.psum(bias_stack.astype(jnp.bfloat16), "dp").astype(jnp.float32),
    )
    return (current_state[None], adjoint[None], kernel_stack, bias_stack)


def solution(mesh):
    in_specs = (
        P("layer", "dp", None, None, None),
        P("layer", None, None, None),
        P("layer", None),
        P("layer", "dp", None, None, None),
    )
    out_specs = (
        P("layer", "dp", None, None, None),
        P("layer", "dp", None, None, None),
        P("layer", None, None, None),
        P("layer", None),
    )
    return jax.shard_map(local, mesh=mesh, in_specs=in_specs, out_specs=out_specs, check_vma=False)
```

profile of v0, /device:TPU:32, one launch (start us, length us, event | category | flops | bytes accessed | tf_op | source)
XLA Modules:
  0.0 527.7 jit_solution(16567710539062359884)
XLA Ops:
  22.3 178.5 %while.30 = (s32[]{:T(128)}, f32[1,32,32,128]{3,2,1,0:T(8,128)S(1)}, s32[]{:T(128)}, bf16[9,128,128]{2,1,0:T(8,128)(2,1)S(1)}, bf16[128]{0:T(256)(128)(2,1)S(1)}, /*index=5*/f32[1,32,32,128]{3,2,1,0:T(8,128)S(1)}, s32[]{:T(128)}) while((s32[]{:T(128)}, f32[1,32,32,128]{3,2,1,0:T(8,128)S(1)}, s32[]{:T(128)}, ...), condition=%wide.region_3.4_spmd, body=%wide.region_0.3_spmd.sunk | while | flops 303693952 | bytes 22578640 | solution.py:105
  25.1 8.8 %collective-permute-done = f32[1,32,32,128]{3,2,1,0:T(8,128)S(1)} collective-permute-done((f32[1,32,32,128]{3,2,1,0:T(8,128)}, f32[1,32,32,128]{3,2,1,0:T(8,128)S(1)}, u32[]{:S(2)}, u32[]{:S(2)}) %collective-permute-start) | collective-permute-done | bytes 524320 | tf_op jit(solution)/shard_map/while/body/eval_jaxpr/ppermute | solution.py:13
  36.9 8.8 %collective-permute-done = f32[1,32,32,128]{3,2,1,0:T(8,128)S(1)} collective-permute-done((f32[1,32,32,128]{3,2,1,0:T(8,128)}, f32[1,32,32,128]{3,2,1,0:T(8,128)S(1)}, u32[]{:S(2)}, u32[]{:S(2)}) %collective-permute-start) | collective-permute-done | bytes 524320 | tf_op jit(solution)/shard_map/while/body/eval_jaxpr/ppermute | solution.py:13
  45.8 2.5 conditional.4
  51.0 8.8 %collective-permute-done = f32[1,32,32,128]{3,2,1,0:T(8,128)S(1)} collective-permute-done((f32[1,32,32,128]{3,2,1,0:T(8,128)}, f32[1,32,32,128]{3,2,1,0:T(8,128)S(1)}, u32[]{:S(2)}, u32[]{:S(2)}) %collective-permute-start) | collective-permute-done | bytes 524320 | tf_op jit(solution)/shard_map/while/body/eval_jaxpr/ppermute | solution.py:13
  62.8 8.8 %collective-permute-done = f32[1,32,32,128]{3,2,1,0:T(8,128)S(1)} collective-permute-done((f32[1,32,32,128]{3,2,1,0:T(8,128)}, f32[1,32,32,128]{3,2,1,0:T(8,128)S(1)}, u32[]{:S(2)}, u32[]{:S(2)}) %collective-permute-start) | collective-permute-done | bytes 524320 | tf_op jit(solution)/shard_map/while/body/eval_jaxpr/ppermute | solution.py:13
  72.6 1.9 collective-permute-start
  74.5 8.8 %collective-permute-done = f32[1,32,32,128]{3,2,1,0:T(8,128)S(1)} collective-permute-done((f32[1,32,32,128]{3,2,1,0:T(8,128)}, f32[1,32,32,128]{3,2,1,0:T(8,128)S(1)}, u32[]{:S(2)}, u32[]{:S(2)}) %collective-permute-start) | collective-permute-done | bytes 524320 | tf_op jit(solution)/shard_map/while/body/eval_jaxpr/ppermute | solution.py:13
  84.3 1.9 collective-permute-start
  86.2 8.8 %collective-permute-done = f32[1,32,32,128]{3,2,1,0:T(8,128)S(1)} collective-permute-done((f32[1,32,32,128]{3,2,1,0:T(8,128)}, f32[1,32,32,128]{3,2,1,0:T(8,128)S(1)}, u32[]{:S(2)}, u32[]{:S(2)}) %collective-permute-start) | collective-permute-done | bytes 524320 | tf_op jit(solution)/shard_map/while/body/eval_jaxpr/ppermute | solution.py:13
  96.0 1.9 collective-permute-start
  98.0 8.8 %collective-permute-done = f32[1,32,32,128]{3,2,1,0:T(8,128)S(1)} collective-permute-done((f32[1,32,32,128]{3,2,1,0:T(8,128)}, f32[1,32,32,128]{3,2,1,0:T(8,128)S(1)}, u32[]{:S(2)}, u32[]{:S(2)}) %collective-permute-start) | collective-permute-done | bytes 524320 | tf_op jit(solution)/shard_map/while/body/eval_jaxpr/ppermute | solution.py:13
  107.8 1.9 collective-permute-start
  109.7 8.8 %collective-permute-done = f32[1,32,32,128]{3,2,1,0:T(8,128)S(1)} collective-permute-done((f32[1,32,32,128]{3,2,1,0:T(8,128)}, f32[1,32,32,128]{3,2,1,0:T(8,128)S(1)}, u32[]{:S(2)}, u32[]{:S(2)}) %collective-permute-start) | collective-permute-done | bytes 524320 | tf_op jit(solution)/shard_map/while/body/eval_jaxpr/ppermute | solution.py:13
  119.5 1.9 collective-permute-start
  121.4 8.8 %collective-permute-done = f32[1,32,32,128]{3,2,1,0:T(8,128)S(1)} collective-permute-done((f32[1,32,32,128]{3,2,1,0:T(8,128)}, f32[1,32,32,128]{3,2,1,0:T(8,128)S(1)}, u32[]{:S(2)}, u32[]{:S(2)}) %collective-permute-start) | collective-permute-done | bytes 524320 | tf_op jit(solution)/shard_map/while/body/eval_jaxpr/ppermute | solution.py:13
  131.2 1.9 collective-permute-start
  133.1 8.8 %collective-permute-done = f32[1,32,32,128]{3,2,1,0:T(8,128)S(1)} collective-permute-done((f32[1,32,32,128]{3,2,1,0:T(8,128)}, f32[1,32,32,128]{3,2,1,0:T(8,128)S(1)}, u32[]{:S(2)}, u32[]{:S(2)}) %collective-permute-start) | collective-permute-done | bytes 524320 | tf_op jit(solution)/shard_map/while/body/eval_jaxpr/ppermute | solution.py:13
  142.9 1.9 collective-permute-start
  144.9 8.8 %collective-permute-done = f32[1,32,32,128]{3,2,1,0:T(8,128)S(1)} collective-permute-done((f32[1,32,32,128]{3,2,1,0:T(8,128)}, f32[1,32,32,128]{3,2,1,0:T(8,128)S(1)}, u32[]{:S(2)}, u32[]{:S(2)}) %collective-permute-start) | collective-permute-done | bytes 524320 | tf_op jit(solution)/shard_map/while/body/eval_jaxpr/ppermute | solution.py:13
  156.6 8.8 %collective-permute-done = f32[1,32,32,128]{3,2,1,0:T(8,128)S(1)} collective-permute-done((f32[1,32,32,128]{3,2,1,0:T(8,128)}, f32[1,32,32,128]{3,2,1,0:T(8,128)S(1)}, u32[]{:S(2)}, u32[]{:S(2)}) %collective-permute-start) | collective-permute-done | bytes 524320 | tf_op jit(solution)/shard_map/while/body/eval_jaxpr/ppermute | solution.py:13
  168.3 8.8 %collective-permute-done = f32[1,32,32,128]{3,2,1,0:T(8,128)S(1)} collective-permute-done((f32[1,32,32,128]{3,2,1,0:T(8,128)}, f32[1,32,32,128]{3,2,1,0:T(8,128)S(1)}, u32[]{:S(2)}, u32[]{:S(2)}) %collective-permute-start) | collective-permute-done | bytes 524320 | tf_op jit(solution)/shard_map/while/body/eval_jaxpr/ppermute | solution.py:13
  180.0 8.8 %collective-permute-done = f32[1,32,32,128]{3,2,1,0:T(8,128)S(1)} collective-permute-done((f32[1,32,32,128]{3,2,1,0:T(8,128)}, f32[1,32,32,128]{3,2,1,0:T(8,128)S(1)}, u32[]{:S(2)}, u32[]{:S(2)}) %collective-permute-start) | collective-permute-done | bytes 524320 | tf_op jit(solution)/shard_map/while/body/eval_jaxpr/ppermute | solution.py:13
  191.8 8.8 %collective-permute-done = f32[1,32,32,128]{3,2,1,0:T(8,128)S(1)} collective-permute-done((f32[1,32,32,128]{3,2,1,0:T(8,128)}, f32[1,32,32,128]{3,2,1,0:T(8,128)S(1)}, u32[]{:S(2)}, u32[]{:S(2)}) %collective-permute-start) | collective-permute-done | bytes 524320 | tf_op jit(solution)/shard_map/while/body/eval_jaxpr/ppermute | solution.py:13
  223.7 168.4 %while.31 = (s32[]{:T(128)}, f32[1,32,32,128]{3,2,1,0:T(8,128)S(1)}, s32[]{:T(128)}, f32[1,32,32,128]{3,2,1,0:T(8,128)S(1)}, f32[1,32,32,128]{3,2,1,0:T(8,128)S(...) while((s32[]{:T(128)}, ...), condition=%wide.region_7.8_spmd, body=%wide.region_4.7_spmd.sunk | while | flops 304087040 | bytes 23626020 | solution.py:136
  226.4 4.2 collective-permute-done.1
  231.5 3.7 collective-permute-start.1
  235.2 4.2 collective-permute-done.1
  240.3 3.7 collective-permute-start.1
  244.0 4.7 collective-permute-done.1
  249.6 3.2 collective-permute-start.1
  252.8 6.6 %collective-permute-done.1 = bf16[1,32,32,128]{3,2,1,0:T(8,128)(2,1)S(1)} collective-permute-done((bf16[1,32,32,128]{3,2,1,0:T(8,128)(2,1)}, bf16[1,32,32,128]{3,2,1,0:T(8,128)(2,1)S(1)}, u32[]{:S(2)}, u32[]{:S(2)}) %collective-permute-start.1) | collective-permute-done | bytes 262176 | tf_op jit(solution)/shard_map/while/body/eval_jaxpr/ppermute | solution.py:13
  262.2 9.5 %collective-permute-done.1 = bf16[1,32,32,128]{3,2,1,0:T(8,128)(2,1)S(1)} collective-permute-done((bf16[1,32,32,128]{3,2,1,0:T(8,128)(2,1)}, bf16[1,32,32,128]{3,2,1,0:T(8,128)(2,1)S(1)}, u32[]{:S(2)}, u32[]{:S(2)}) %collective-permute-start.1) | collective-permute-done | bytes 262176 | tf_op jit(solution)/shard_map/while/body/eval_jaxpr/ppermute | solution.py:13
  274.6 7.8 %collective-permute-done.1 = bf16[1,32,32,128]{3,2,1,0:T(8,128)(2,1)S(1)} collective-permute-done((bf16[1,32,32,128]{3,2,1,0:T(8,128)(2,1)}, bf16[1,32,32,128]{3,2,1,0:T(8,128)(2,1)S(1)}, u32[]{:S(2)}, u32[]{:S(2)}) %collective-permute-start.1) | collective-permute-done | bytes 262176 | tf_op jit(solution)/shard_map/while/body/eval_jaxpr/ppermute | solution.py:13
  285.2 7.2 %collective-permute-done.1 = bf16[1,32,32,128]{3,2,1,0:T(8,128)(2,1)S(1)} collective-permute-done((bf16[1,32,32,128]{3,2,1,0:T(8,128)(2,1)}, bf16[1,32,32,128]{3,2,1,0:T(8,128)(2,1)S(1)}, u32[]{:S(2)}, u32[]{:S(2)}) %collective-permute-start.1) | collective-permute-done | bytes 262176 | tf_op jit(solution)/shard_map/while/body/eval_jaxpr/ppermute | solution.py:13
  295.3 7.2 %collective-permute-done.1 = bf16[1,32,32,128]{3,2,1,0:T(8,128)(2,1)S(1)} collective-permute-done((bf16[1,32,32,128]{3,2,1,0:T(8,128)(2,1)}, bf16[1,32,32,128]{3,2,1,0:T(8,128)(2,1)S(1)}, u32[]{:S(2)}, u32[]{:S(2)}) %collective-permute-start.1) | collective-permute-done | bytes 262176 | tf_op jit(solution)/shard_map/while/body/eval_jaxpr/ppermute | solution.py:13
  305.3 7.2 %collective-permute-done.1 = bf16[1,32,32,128]{3,2,1,0:T(8,128)(2,1)S(1)} collective-permute-done((bf16[1,32,32,128]{3,2,1,0:T(8,128)(2,1)}, bf16[1,32,32,128]{3,2,1,0:T(8,128)(2,1)S(1)}, u32[]{:S(2)}, u32[]{:S(2)}) %collective-permute-start.1) | collective-permute-done | bytes 262176 | tf_op jit(solution)/shard_map/while/body/eval_jaxpr/ppermute | solution.py:13
  315.3 7.2 %collective-permute-done.1 = bf16[1,32,32,128]{3,2,1,0:T(8,128)(2,1)S(1)} collective-permute-done((bf16[1,32,32,128]{3,2,1,0:T(8,128)(2,1)}, bf16[1,32,32,128]{3,2,1,0:T(8,128)(2,1)S(1)}, u32[]{:S(2)}, u32[]{:S(2)}) %collective-permute-start.1) | collective-permute-done | bytes 262176 | tf_op jit(solution)/shard_map/while/body/eval_jaxpr/ppermute | solution.py:13
  325.4 7.2 %collective-permute-done.1 = bf16[1,32,32,128]{3,2,1,0:T(8,128)(2,1)S(1)} collective-permute-done((bf16[1,32,32,128]{3,2,1,0:T(8,128)(2,1)}, bf16[1,32,32,128]{3,2,1,0:T(8,128)(2,1)S(1)}, u32[]{:S(2)}, u32[]{:S(2)}) %collective-permute-start.1) | collective-permute-done | bytes 262176 | tf_op jit(solution)/shard_map/while/body/eval_jaxpr/ppermute | solution.py:13
  335.4 7.2 %collective-permute-done.1 = bf16[1,32,32,128]{3,2,1,0:T(8,128)(2,1)S(1)} collective-permute-done((bf16[1,32,32,128]{3,2,1,0:T(8,128)(2,1)}, bf16[1,32,32,128]{3,2,1,0:T(8,128)(2,1)S(1)}, u32[]{:S(2)}, u32[]{:S(2)}) %collective-permute-start.1) | collective-permute-done | bytes 262176 | tf_op jit(solution)/shard_map/while/body/eval_jaxpr/ppermute | solution.py:13
  345.4 23.9 %collective-permute-done.1 = bf16[1,32,32,128]{3,2,1,0:T(8,128)(2,1)S(1)} collective-permute-done((bf16[1,32,32,128]{3,2,1,0:T(8,128)(2,1)}, bf16[1,32,32,128]{3,2,1,0:T(8,128)(2,1)S(1)}, u32[]{:S(2)}, u32[]{:S(2)}) %collective-permute-start.1) | collective-permute-done | bytes 262176 | tf_op jit(solution)/shard_map/while/body/eval_jaxpr/ppermute | solution.py:13
  369.5 3.3 conditional.5
  375.4 4.2 collective-permute-done.1
  380.6 7.0 %collective-permute-start.1 = (bf16[1,32,32,128]{3,2,1,0:T(8,128)(2,1)}, bf16[1,32,32,128]{3,2,1,0:T(8,128)(2,1)S(1)}, u32[]{:S(2)}, u32[]{:S(2)}) collective-permute-start(bf16[1,32,32,128]{3,2,1,0:T(8,128)(2,1)} %copy-done.12), channel_id=1, source_target_pairs={{16,0},{32,16},{48,32},{64,48},{80,64},{96,80},{112,96},{128,112},... | collective-permute-start | bytes 786440 | tf_op jit(solution)/shard_map/while/body/eval_jaxpr/ppermute | solution.py:13
  387.6 4.2 collective-permute-done.1
  417.9 40.9 %psum.15 = bf16[4,128]{1,0:T(4,128)(2,1)S(1)} all-reduce(bf16[4,128]{1,0:T(4,128)(2,1)S(1)} %pad_maximum_fusion.1), channel_id=1, replica_groups=mesh['layer'=16,'dp'=16] {'dp'}, use_global_device_ids=true, to_apply=%region_13.14 | all-reduce | flops 512 | bytes 2048 | tf_op jit(solution)/shard_map/psum | solution.py:151
  464.4 53.4 %all-reduce.20.cloned.1.call-done = bf16[4,9,128,128]{3,2,1,0:T(8,128)(2,1)} async-done(((bf16[4,9,128,128]{3,2,1,0:T(8,128)(2,1)}), bf16[4,9,128,128]{3,2,1,0:T(8,128)(2,1)}) %all-reduce.20.cloned.1.call-update) | async-done | bytes 1179664 | tf_op jit(solution)/shard_map/psum | solution.py:150
  517.9 3.0 convert_element_type.313
  (479 shorter events, 138.6 us)
Async XLA Ops:
  7.2 510.7 %all-reduce.20.cloned.1.call-start = ((), (), s32[]{:S(2)}) async-start(), calls=%async_computation | async-start | bytes 2359296 | tf_op jit(solution)/shard_map/psum | solution.py:150
  8.3 1.3 copy-start.1
  12.0 2.4 copy-start.10
  14.7 2.3 copy-start.15
  19.3 1.2 copy-start.31
  19.3 1.5 copy-start.29
  20.8 1.2 copy-start.16
  23.2 10.7 %collective-permute-start = (f32[1,32,32,128]{3,2,1,0:T(8,128)}, f32[1,32,32,128]{3,2,1,0:T(8,128)S(1)}, u32[]{:S(2)}, u32[]{:S(2)}) collective-permute-start(f32[1,32,32,128]{3,2,1,0:T(8,128)} %copy-done.5), channel_id=1, source_target_pairs={{0,16},{16,32},{32,48},{48,64},{64,80},{80,96},{96,112},{112,128},... | collective-permute-start | bytes 1572872 | tf_op jit(solution)/shard_map/while/body/eval_jaxpr/ppermute | solution.py:13
  34.9 10.8 %collective-permute-start = (f32[1,32,32,128]{3,2,1,0:T(8,128)}, f32[1,32,32,128]{3,2,1,0:T(8,128)S(1)}, u32[]{:S(2)}, u32[]{:S(2)}) collective-permute-start(f32[1,32,32,128]{3,2,1,0:T(8,128)} %copy-done.5), channel_id=1, source_target_pairs={{0,16},{16,32},{32,48},{48,64},{64,80},{80,96},{96,112},{112,128},... | collective-permute-start | bytes 1572872 | tf_op jit(solution)/shard_map/while/body/eval_jaxpr/ppermute | solution.py:13
  49.1 10.7 %collective-permute-start = (f32[1,32,32,128]{3,2,1,0:T(8,128)}, f32[1,32,32,128]{3,2,1,0:T(8,128)S(1)}, u32[]{:S(2)}, u32[]{:S(2)}) collective-permute-start(f32[1,32,32,128]{3,2,1,0:T(8,128)} %copy-done.5), channel_id=1, source_target_pairs={{0,16},{16,32},{32,48},{48,64},{64,80},{80,96},{96,112},{112,128},... | collective-permute-start | bytes 1572872 | tf_op jit(solution)/shard_map/while/body/eval_jaxpr/ppermute | solution.py:13
  60.8 10.7 %collective-permute-start = (f32[1,32,32,128]{3,2,1,0:T(8,128)}, f32[1,32,32,128]{3,2,1,0:T(8,128)S(1)}, u32[]{:S(2)}, u32[]{:S(2)}) collective-permute-start(f32[1,32,32,128]{3,2,1,0:T(8,128)} %copy-done.5), channel_id=1, source_target_pairs={{0,16},{16,32},{32,48},{48,64},{64,80},{80,96},{96,112},{112,128},... | collective-permute-start | bytes 1572872 | tf_op jit(solution)/shard_map/while/body/eval_jaxpr/ppermute | solution.py:13
  72.6 10.7 %collective-permute-start = (f32[1,32,32,128]{3,2,1,0:T(8,128)}, f32[1,32,32,128]{3,2,1,0:T(8,128)S(1)}, u32[]{:S(2)}, u32[]{:S(2)}) collective-permute-start(f32[1,32,32,128]{3,2,1,0:T(8,128)} %copy-done.5), channel_id=1, source_target_pairs={{0,16},{16,32},{32,48},{48,64},{64,80},{80,96},{96,112},{112,128},... | collective-permute-start | bytes 1572872 | tf_op jit(solution)/shard_map/while/body/eval_jaxpr/ppermute | solution.py:13
  84.3 10.7 %collective-permute-start = (f32[1,32,32,128]{3,2,1,0:T(8,128)}, f32[1,32,32,128]{3,2,1,0:T(8,128)S(1)}, u32[]{:S(2)}, u32[]{:S(2)}) collective-permute-start(f32[1,32,32,128]{3,2,1,0:T(8,128)} %copy-done.5), channel_id=1, source_target_pairs={{0,16},{16,32},{32,48},{48,64},{64,80},{80,96},{96,112},{112,128},... | collective-permute-start | bytes 1572872 | tf_op jit(solution)/shard_map/while/body/eval_jaxpr/ppermute | solution.py:13
  96.0 10.7 %collective-permute-start = (f32[1,32,32,128]{3,2,1,0:T(8,128)}, f32[1,32,32,128]{3,2,1,0:T(8,128)S(1)}, u32[]{:S(2)}, u32[]{:S(2)}) collective-permute-start(f32[1,32,32,128]{3,2,1,0:T(8,128)} %copy-done.5), channel_id=1, source_target_pairs={{0,16},{16,32},{32,48},{48,64},{64,80},{80,96},{96,112},{112,128},... | collective-permute-start | bytes 1572872 | tf_op jit(solution)/shard_map/while/body/eval_jaxpr/ppermute | solution.py:13
  107.8 10.7 %collective-permute-start = (f32[1,32,32,128]{3,2,1,0:T(8,128)}, f32[1,32,32,128]{3,2,1,0:T(8,128)S(1)}, u32[]{:S(2)}, u32[]{:S(2)}) collective-permute-start(f32[1,32,32,128]{3,2,1,0:T(8,128)} %copy-done.5), channel_id=1, source_target_pairs={{0,16},{16,32},{32,48},{48,64},{64,80},{80,96},{96,112},{112,128},... | collective-permute-start | bytes 1572872 | tf_op jit(solution)/shard_map/while/body/eval_jaxpr/ppermute | solution.py:13
  119.5 10.7 %collective-permute-start = (f32[1,32,32,128]{3,2,1,0:T(8,128)}, f32[1,32,32,128]{3,2,1,0:T(8,128)S(1)}, u32[]{:S(2)}, u32[]{:S(2)}) collective-permute-start(f32[1,32,32,128]{3,2,1,0:T(8,128)} %copy-done.5), channel_id=1, source_target_pairs={{0,16},{16,32},{32,48},{48,64},{64,80},{80,96},{96,112},{112,128},... | collective-permute-start | bytes 1572872 | tf_op jit(solution)/shard_map/while/body/eval_jaxpr/ppermute | solution.py:13
  131.2 10.7 %collective-permute-start = (f32[1,32,32,128]{3,2,1,0:T(8,128)}, f32[1,32,32,128]{3,2,1,0:T(8,128)S(1)}, u32[]{:S(2)}, u32[]{:S(2)}) collective-permute-start(f32[1,32,32,128]{3,2,1,0:T(8,128)} %copy-done.5), channel_id=1, source_target_pairs={{0,16},{16,32},{32,48},{48,64},{64,80},{80,96},{96,112},{112,128},... | collective-permute-start | bytes 1572872 | tf_op jit(solution)/shard_map/while/body/eval_jaxpr/ppermute | solution.py:13
  142.9 10.7 %collective-permute-start = (f32[1,32,32,128]{3,2,1,0:T(8,128)}, f32[1,32,32,128]{3,2,1,0:T(8,128)S(1)}, u32[]{:S(2)}, u32[]{:S(2)}) collective-permute-start(f32[1,32,32,128]{3,2,1,0:T(8,128)} %copy-done.5), channel_id=1, source_target_pairs={{0,16},{16,32},{32,48},{48,64},{64,80},{80,96},{96,112},{112,128},... | collective-permute-start | bytes 1572872 | tf_op jit(solution)/shard_map/while/body/eval_jaxpr/ppermute | solution.py:13
  154.7 10.7 %collective-permute-start = (f32[1,32,32,128]{3,2,1,0:T(8,128)}, f32[1,32,32,128]{3,2,1,0:T(8,128)S(1)}, u32[]{:S(2)}, u32[]{:S(2)}) collective-permute-start(f32[1,32,32,128]{3,2,1,0:T(8,128)} %copy-done.5), channel_id=1, source_target_pairs={{0,16},{16,32},{32,48},{48,64},{64,80},{80,96},{96,112},{112,128},... | collective-permute-start | bytes 1572872 | tf_op jit(solution)/shard_map/while/body/eval_jaxpr/ppermute | solution.py:13
  166.4 10.7 %collective-permute-start = (f32[1,32,32,128]{3,2,1,0:T(8,128)}, f32[1,32,32,128]{3,2,1,0:T(8,128)S(1)}, u32[]{:S(2)}, u32[]{:S(2)}) collective-permute-start(f32[1,32,32,128]{3,2,1,0:T(8,128)} %copy-done.5), channel_id=1, source_target_pairs={{0,16},{16,32},{32,48},{48,64},{64,80},{80,96},{96,112},{112,128},... | collective-permute-start | bytes 1572872 | tf_op jit(solution)/shard_map/while/body/eval_jaxpr/ppermute | solution.py:13
  178.1 10.7 %collective-permute-start = (f32[1,32,32,128]{3,2,1,0:T(8,128)}, f32[1,32,32,128]{3,2,1,0:T(8,128)S(1)}, u32[]{:S(2)}, u32[]{:S(2)}) collective-permute-start(f32[1,32,32,128]{3,2,1,0:T(8,128)} %copy-done.5), channel_id=1, source_target_pairs={{0,16},{16,32},{32,48},{48,64},{64,80},{80,96},{96,112},{112,128},... | collective-permute-start | bytes 1572872 | tf_op jit(solution)/shard_map/while/body/eval_jaxpr/ppermute | solution.py:13
  189.8 10.7 %collective-permute-start = (f32[1,32,32,128]{3,2,1,0:T(8,128)}, f32[1,32,32,128]{3,2,1,0:T(8,128)S(1)}, u32[]{:S(2)}, u32[]{:S(2)}) collective-permute-start(f32[1,32,32,128]{3,2,1,0:T(8,128)} %copy-done.5), channel_id=1, source_target_pairs={{0,16},{16,32},{32,48},{48,64},{64,80},{80,96},{96,112},{112,128},... | collective-permute-start | bytes 1572872 | tf_op jit(solution)/shard_map/while/body/eval_jaxpr/ppermute | solution.py:13
  200.9 1.2 copy-start.17
  203.3 1.2 copy-start.19
  205.6 13.2 %copy-start.6 = (f32[1024,128]{1,0:T(8,128)}, f32[1024,128]{1,0:T(8,128)S(1)}, u32[]{:S(2)}) copy-start(f32[1024,128]{1,0:T(8,128)S(1)} %convolution_add_fusion.96) | copy-start | bytes 1572868
  205.8 1.2 copy-start.21
  205.8 2.3 copy-start.13
  208.1 7.9 %copy-start.3 = (f32[1024,128]{1,0:T(8,128)}, f32[1024,128]{1,0:T(8,128)S(1)}, u32[]{:S(2)}) copy-start(f32[1024,128]{1,0:T(8,128)S(1)} %convolution_add_fusion.88) | copy-start | bytes 1572868
  208.2 1.2 copy-start.23
  224.4 6.1 %collective-permute-start.1 = (bf16[1,32,32,128]{3,2,1,0:T(8,128)(2,1)}, bf16[1,32,32,128]{3,2,1,0:T(8,128)(2,1)S(1)}, u32[]{:S(2)}, u32[]{:S(2)}) collective-permute-start(bf16[1,32,32,128]{3,2,1,0:T(8,128)(2,1)} %copy-done.12), channel_id=1, source_target_pairs={{16,0},{32,16},{48,32},{64,48},{80,64},{96,80},{112,96},{128,112},... | collective-permute-start | bytes 786440 | tf_op jit(solution)/shard_map/while/body/eval_jaxpr/ppermute | solution.py:13
  231.5 7.9 %collective-permute-start.1 = (bf16[1,32,32,128]{3,2,1,0:T(8,128)(2,1)}, bf16[1,32,32,128]{3,2,1,0:T(8,128)(2,1)S(1)}, u32[]{:S(2)}, u32[]{:S(2)}) collective-permute-start(bf16[1,32,32,128]{3,2,1,0:T(8,128)(2,1)} %copy-done.12), channel_id=1, source_target_pairs={{16,0},{32,16},{48,32},{64,48},{80,64},{96,80},{112,96},{128,112},... | collective-permute-start | bytes 786440 | tf_op jit(solution)/shard_map/while/body/eval_jaxpr/ppermute | solution.py:13
  240.3 8.4 %collective-permute-start.1 = (bf16[1,32,32,128]{3,2,1,0:T(8,128)(2,1)}, bf16[1,32,32,128]{3,2,1,0:T(8,128)(2,1)S(1)}, u32[]{:S(2)}, u32[]{:S(2)}) collective-permute-start(bf16[1,32,32,128]{3,2,1,0:T(8,128)(2,1)} %copy-done.12), channel_id=1, source_target_pairs={{16,0},{32,16},{48,32},{64,48},{80,64},{96,80},{112,96},{128,112},... | collective-permute-start | bytes 786440 | tf_op jit(solution)/shard_map/while/body/eval_jaxpr/ppermute | solution.py:13
  249.6 9.8 %collective-permute-start.1 = (bf16[1,32,32,128]{3,2,1,0:T(8,128)(2,1)}, bf16[1,32,32,128]{3,2,1,0:T(8,128)(2,1)S(1)}, u32[]{:S(2)}, u32[]{:S(2)}) collective-permute-start(bf16[1,32,32,128]{3,2,1,0:T(8,128)(2,1)} %copy-done.12), channel_id=1, source_target_pairs={{16,0},{32,16},{48,32},{64,48},{80,64},{96,80},{112,96},{128,112},... | collective-permute-start | bytes 786440 | tf_op jit(solution)/shard_map/while/body/eval_jaxpr/ppermute | solution.py:13
  260.3 11.4 %collective-permute-start.1 = (bf16[1,32,32,128]{3,2,1,0:T(8,128)(2,1)}, bf16[1,32,32,128]{3,2,1,0:T(8,128)(2,1)S(1)}, u32[]{:S(2)}, u32[]{:S(2)}) collective-permute-start(bf16[1,32,32,128]{3,2,1,0:T(8,128)(2,1)} %copy-done.12), channel_id=1, source_target_pairs={{16,0},{32,16},{48,32},{64,48},{80,64},{96,80},{112,96},{128,112},... | collective-permute-start | bytes 786440 | tf_op jit(solution)/shard_map/while/body/eval_jaxpr/ppermute | solution.py:13
  272.6 9.7 %collective-permute-start.1 = (bf16[1,32,32,128]{3,2,1,0:T(8,128)(2,1)}, bf16[1,32,32,128]{3,2,1,0:T(8,128)(2,1)S(1)}, u32[]{:S(2)}, u32[]{:S(2)}) collective-permute-start(bf16[1,32,32,128]{3,2,1,0:T(8,128)(2,1)} %copy-done.12), channel_id=1, source_target_pairs={{16,0},{32,16},{48,32},{64,48},{80,64},{96,80},{112,96},{128,112},... | collective-permute-start | bytes 786440 | tf_op jit(solution)/shard_map/while/body/eval_jaxpr/ppermute | solution.py:13
  283.3 9.1 %collective-permute-start.1 = (bf16[1,32,32,128]{3,2,1,0:T(8,128)(2,1)}, bf16[1,32,32,128]{3,2,1,0:T(8,128)(2,1)S(1)}, u32[]{:S(2)}, u32[]{:S(2)}) collective-permute-start(bf16[1,32,32,128]{3,2,1,0:T(8,128)(2,1)} %copy-done.12), channel_id=1, source_target_pairs={{16,0},{32,16},{48,32},{64,48},{80,64},{96,80},{112,96},{128,112},... | collective-permute-start | bytes 786440 | tf_op jit(solution)/shard_map/while/body/eval_jaxpr/ppermute | solution.py:13
  293.3 9.1 %collective-permute-start.1 = (bf16[1,32,32,128]{3,2,1,0:T(8,128)(2,1)}, bf16[1,32,32,128]{3,2,1,0:T(8,128)(2,1)S(1)}, u32[]{:S(2)}, u32[]{:S(2)}) collective-permute-start(bf16[1,32,32,128]{3,2,1,0:T(8,128)(2,1)} %copy-done.12), channel_id=1, source_target_pairs={{16,0},{32,16},{48,32},{64,48},{80,64},{96,80},{112,96},{128,112},... | collective-permute-start | bytes 786440 | tf_op jit(solution)/shard_map/while/body/eval_jaxpr/ppermute | solution.py:13
  303.4 9.1 %collective-permute-start.1 = (bf16[1,32,32,128]{3,2,1,0:T(8,128)(2,1)}, bf16[1,32,32,128]{3,2,1,0:T(8,128)(2,1)S(1)}, u32[]{:S(2)}, u32[]{:S(2)}) collective-permute-start(bf16[1,32,32,128]{3,2,1,0:T(8,128)(2,1)} %copy-done.12), channel_id=1, source_target_pairs={{16,0},{32,16},{48,32},{64,48},{80,64},{96,80},{112,96},{128,112},... | collective-permute-start | bytes 786440 | tf_op jit(solution)/shard_map/while/body/eval_jaxpr/ppermute | solution.py:13
  313.4 9.1 %collective-permute-start.1 = (bf16[1,32,32,128]{3,2,1,0:T(8,128)(2,1)}, bf16[1,32,32,128]{3,2,1,0:T(8,128)(2,1)S(1)}, u32[]{:S(2)}, u32[]{:S(2)}) collective-permute-start(bf16[1,32,32,128]{3,2,1,0:T(8,128)(2,1)} %copy-done.12), channel_id=1, source_target_pairs={{16,0},{32,16},{48,32},{64,48},{80,64},{96,80},{112,96},{128,112},... | collective-permute-start | bytes 786440 | tf_op jit(solution)/shard_map/while/body/eval_jaxpr/ppermute | solution.py:13
  323.4 9.1 %collective-permute-start.1 = (bf16[1,32,32,128]{3,2,1,0:T(8,128)(2,1)}, bf16[1,32,32,128]{3,2,1,0:T(8,128)(2,1)S(1)}, u32[]{:S(2)}, u32[]{:S(2)}) collective-permute-start(bf16[1,32,32,128]{3,2,1,0:T(8,128)(2,1)} %copy-done.12), channel_id=1, source_target_pairs={{16,0},{32,16},{48,32},{64,48},{80,64},{96,80},{112,96},{128,112},... | collective-permute-start | bytes 786440 | tf_op jit(solution)/shard_map/while/body/eval_jaxpr/ppermute | solution.py:13
  333.5 9.1 %collective-permute-start.1 = (bf16[1,32,32,128]{3,2,1,0:T(8,128)(2,1)}, bf16[1,32,32,128]{3,2,1,0:T(8,128)(2,1)S(1)}, u32[]{:S(2)}, u32[]{:S(2)}) collective-permute-start(bf16[1,32,32,128]{3,2,1,0:T(8,128)(2,1)} %copy-done.12), channel_id=1, source_target_pairs={{16,0},{32,16},{48,32},{64,48},{80,64},{96,80},{112,96},{128,112},... | collective-permute-start | bytes 786440 | tf_op jit(solution)/shard_map/while/body/eval_jaxpr/ppermute | solution.py:13
  343.5 25.8 %collective-permute-start.1 = (bf16[1,32,32,128]{3,2,1,0:T(8,128)(2,1)}, bf16[1,32,32,128]{3,2,1,0:T(8,128)(2,1)S(1)}, u32[]{:S(2)}, u32[]{:S(2)}) collective-permute-start(bf16[1,32,32,128]{3,2,1,0:T(8,128)(2,1)} %copy-done.12), channel_id=1, source_target_pairs={{16,0},{32,16},{48,32},{64,48},{80,64},{96,80},{112,96},{128,112},... | collective-permute-start | bytes 786440 | tf_op jit(solution)/shard_map/while/body/eval_jaxpr/ppermute | solution.py:13
  373.5 6.1 %collective-permute-start.1 = (bf16[1,32,32,128]{3,2,1,0:T(8,128)(2,1)}, bf16[1,32,32,128]{3,2,1,0:T(8,128)(2,1)S(1)}, u32[]{:S(2)}, u32[]{:S(2)}) collective-permute-start(bf16[1,32,32,128]{3,2,1,0:T(8,128)(2,1)} %copy-done.12), channel_id=1, source_target_pairs={{16,0},{32,16},{48,32},{64,48},{80,64},{96,80},{112,96},{128,112},... | collective-permute-start | bytes 786440 | tf_op jit(solution)/shard_map/while/body/eval_jaxpr/ppermute | solution.py:13
  380.6 11.2 %collective-permute-start.1 = (bf16[1,32,32,128]{3,2,1,0:T(8,128)(2,1)}, bf16[1,32,32,128]{3,2,1,0:T(8,128)(2,1)S(1)}, u32[]{:S(2)}, u32[]{:S(2)}) collective-permute-start(bf16[1,32,32,128]{3,2,1,0:T(8,128)(2,1)} %copy-done.12), channel_id=1, source_target_pairs={{16,0},{32,16},{48,32},{64,48},{80,64},{96,80},{112,96},{128,112},... | collective-permute-start | bytes 786440 | tf_op jit(solution)/shard_map/while/body/eval_jaxpr/ppermute | solution.py:13
  395.3 1.3 copy-start.14
  401.0 1.2 copy-start.22
  458.9 2.0 copy-start.30
  459.7 1.5 copy-start.28
  (44 other events, 36.4 us)
Sparse Core Ops, SparseCore 0:
  416.7 101.0 all-reduce.19
where the time goes:
time: 529 us; the launch traced here: 528 us
  waiting for transfers between devices  297 us (56%)
  starting transfers between devices  67.2 us (13%)
  matrix products  47.4 us (9%)
  blocking collectives  40.9 us (8%)
  local copies, waits for them, and re-layouts  40.5 us (8%)
  between operations  15.9 us (3%)
  other arithmetic  15.6 us (3%)
    ppermute x30, waiting for transfers between devices, passed_along(): return lax.ppermute(x, axis, pairs)  244 us
    ppermute x30, starting transfers between devices, passed_along(): return lax.ppermute(x, axis, pairs)  67.2 us
    psum x1, waiting for transfers between devices, local(): lax.psum(kernel_stack.astype(jnp.bfloat16), 'dp').astype(jnp.float32)  53.4 us
    psum x1, blocking collectives, local(): lax.psum(bias_stack.astype(jnp.bfloat16), 'dp').astype(jnp.float32)  40.9 us
    while x60, local copies, waits for them, and re-layouts  22.5 us
    dot_general x81, matrix products, transposed(): lax.dot_general(view, kernel[tap_index], (((1,), (1,)), ((), ())), prefer...  19.6 us
    dot_general x81, matrix products, convolve(): jnp.dot(view, kernel[tap_index], preferred_element_type=jnp.float32)  18.1 us
  transfers between devices with their start and end apart: 31, of which 31 were waited for; matrix products, arithmetic and copies ran while one was open for 1% of the time, Pallas kernels for 0%

commit v1 on v0

--- a/solution.py
+++ b/solution.py
@@ -146,8 +146,9 @@
         adjoint = adjoint + step_size * transposed(signal, weights[inner_pos])
     kernel_stack = jnp.stack(kernel_grads)
     bias_stack = jnp.stack(bias_grads)
+    derive_ranges = lambda mine_x, link_axis: jnp.sum(lax.all_gather(mine_x, link_axis), axis=0)
     kernel_stack, bias_stack = (
-        lax.psum(kernel_stack.astype(jnp.bfloat16), "dp").astype(jnp.float32),
+        derive_ranges(kernel_stack.astype(jnp.bfloat16), "dp").astype(jnp.float32),
         lax.psum(bias_stack.astype(jnp.bfloat16), "dp").astype(jnp.float32),
     )
     return (current_state[None], adjoint[None], kernel_stack, bias_stack)

time: 529 us -> 577 us (1.091); the launches traced: 528 us -> 568 us
  waiting for transfers between devices: 297 us -> 329 us
  other arithmetic: 15.6 us -> 28.4 us
    all_gather x0 -> x1, waiting for transfers between devices: none -> 85 us  [local(): lax.all_gather(mine_x, link_axis)]
    psum x1 -> x0, waiting for transfers between devices: 53.4 us -> none  [local(): lax.psum(kernel_stack.astype(jnp.bfloat16), 'dp').astype(jnp.float32)]
    while x60 -> x30, local copies, waits for them, and re-layouts: 22.5 us -> 10.8 us
    another operation x28, local copies, waits for them, and re-layouts: 1.22 us -> 12.5 us
    reduce_sum x0 -> x1, other arithmetic: none -> 10.6 us  [local(): jnp.sum(lax.all_gather(mine_x, link_axis), axis=0)]
where the time goes in v1:
time: 577 us; the launch traced here: 568 us
  waiting for transfers between devices  329 us (57%)
  starting transfers between devices  68.5 us (12%)
  matrix products  46.1 us (8%)
  blocking collectives  41.7 us (7%)
  local copies, waits for them, and re-layouts  35.5 us (6%)
  other arithmetic  28.4 us (5%)
  between operations  16.2 us (3%)
    ppermute x30, waiting for transfers between devices, passed_along(): return lax.ppermute(x, axis, pairs)  245 us
    all_gather x1, waiting for transfers between devices, local(): lax.all_gather(mine_x, link_axis)  85 us
    ppermute x30, starting transfers between devices, passed_along(): return lax.ppermute(x, axis, pairs)  68.4 us
    psum x1, blocking collectives, local(): lax.psum(bias_stack.astype(jnp.bfloat16), 'dp').astype(jnp.float32)  41.7 us
    dot_general x81, matrix products, transposed(): lax.dot_general(view, kernel[tap_index], (((1,), (1,)), ((), ())), prefer...  19.3 us
    dot_general x81, matrix products, convolve(): jnp.dot(view, kernel[tap_index], preferred_element_type=jnp.float32)  17.1 us
    another operation x28, local copies, waits for them, and re-layouts  12.5 us
  transfers between devices with their start and end apart: 31, of which 31 were waited for; matrix products, arithmetic and copies ran while one was open for 1% of the time, Pallas kernels for 0%

profile of v1, /device:TPU:32, one launch (start us, length us, event | category | flops | bytes accessed | tf_op | source)
XLA Modules:
  0.0 568.3 jit_solution(1352954768719179598)
XLA Ops:
  20.1 183.3 %while.30 = (s32[]{:T(128)}, f32[1,32,32,128]{3,2,1,0:T(8,128)S(1)}, s32[]{:T(128)}, bf16[9,128,128]{2,1,0:T(8,128)(2,1)S(1)}, bf16[128]{0:T(256)(128)(2,1)S(1)}, /*index=5*/f32[1,32,32,128]{3,2,1,0:T(8,128)}, s32[]{:T(128)}) while((s32[]{:T(128)}, f32[1,32,32,128]{3,2,1,0:T(8,128)S(1)}, s32[]{:T(128)}, bf16[9,128,128]{2,1,0:T(8,128)(2,1)S(1)}, ...), condition=%wide.region_3.4_spmd, body=%wide.region_0.3_spmd.sunk | while | flops 303693952 | bytes 22578640 | solution.py:105
  21.0 1.9 collective-permute-start
  22.9 8.9 %collective-permute-done = f32[1,32,32,128]{3,2,1,0:T(8,128)} collective-permute-done((f32[1,32,32,128]{3,2,1,0:T(8,128)}, f32[1,32,32,128]{3,2,1,0:T(8,128)}, u32[]{:S(2)}, u32[]{:S(2)}) %collective-permute-start) | collective-permute-done | bytes 524320 | tf_op jit(solution)/shard_map/while/body/eval_jaxpr/ppermute | solution.py:13
  32.8 1.9 collective-permute-start
  34.7 10.5 %collective-permute-done = f32[1,32,32,128]{3,2,1,0:T(8,128)} collective-permute-done((f32[1,32,32,128]{3,2,1,0:T(8,128)}, f32[1,32,32,128]{3,2,1,0:T(8,128)}, u32[]{:S(2)}, u32[]{:S(2)}) %collective-permute-start) | collective-permute-done | bytes 524320 | tf_op jit(solution)/shard_map/while/body/eval_jaxpr/ppermute | solution.py:13
  46.4 3.9 conditional.4
  50.3 1.9 collective-permute-start
  52.3 8.9 %collective-permute-done = f32[1,32,32,128]{3,2,1,0:T(8,128)} collective-permute-done((f32[1,32,32,128]{3,2,1,0:T(8,128)}, f32[1,32,32,128]{3,2,1,0:T(8,128)}, u32[]{:S(2)}, u32[]{:S(2)}) %collective-permute-start) | collective-permute-done | bytes 524320 | tf_op jit(solution)/shard_map/while/body/eval_jaxpr/ppermute | solution.py:13
  62.2 1.9 collective-permute-start
  64.1 8.9 %collective-permute-done = f32[1,32,32,128]{3,2,1,0:T(8,128)} collective-permute-done((f32[1,32,32,128]{3,2,1,0:T(8,128)}, f32[1,32,32,128]{3,2,1,0:T(8,128)}, u32[]{:S(2)}, u32[]{:S(2)}) %collective-permute-start) | collective-permute-done | bytes 524320 | tf_op jit(solution)/shard_map/while/body/eval_jaxpr/ppermute | solution.py:13
  74.0 1.9 collective-permute-start
  75.9 8.9 %collective-permute-done = f32[1,32,32,128]{3,2,1,0:T(8,128)} collective-permute-done((f32[1,32,32,128]{3,2,1,0:T(8,128)}, f32[1,32,32,128]{3,2,1,0:T(8,128)}, u32[]{:S(2)}, u32[]{:S(2)}) %collective-permute-start) | collective-permute-done | bytes 524320 | tf_op jit(solution)/shard_map/while/body/eval_jaxpr/ppermute | solution.py:13
  85.8 1.9 collective-permute-start
  87.7 8.9 %collective-permute-done = f32[1,32,32,128]{3,2,1,0:T(8,128)} collective-permute-done((f32[1,32,32,128]{3,2,1,0:T(8,128)}, f32[1,32,32,128]{3,2,1,0:T(8,128)}, u32[]{:S(2)}, u32[]{:S(2)}) %collective-permute-start) | collective-permute-done | bytes 524320 | tf_op jit(solution)/shard_map/while/body/eval_jaxpr/ppermute | solution.py:13
  99.6 8.9 %collective-permute-done = f32[1,32,32,128]{3,2,1,0:T(8,128)} collective-permute-done((f32[1,32,32,128]{3,2,1,0:T(8,128)}, f32[1,32,32,128]{3,2,1,0:T(8,128)}, u32[]{:S(2)}, u32[]{:S(2)}) %collective-permute-start) | collective-permute-done | bytes 524320 | tf_op jit(solution)/shard_map/while/body/eval_jaxpr/ppermute | solution.py:13
  111.4 8.9 %collective-permute-done = f32[1,32,32,128]{3,2,1,0:T(8,128)} collective-permute-done((f32[1,32,32,128]{3,2,1,0:T(8,128)}, f32[1,32,32,128]{3,2,1,0:T(8,128)}, u32[]{:S(2)}, u32[]{:S(2)}) %collective-permute-start) | collective-permute-done | bytes 524320 | tf_op jit(solution)/shard_map/while/body/eval_jaxpr/ppermute | solution.py:13
  123.2 8.9 %collective-permute-done = f32[1,32,32,128]{3,2,1,0:T(8,128)} collective-permute-done((f32[1,32,32,128]{3,2,1,0:T(8,128)}, f32[1,32,32,128]{3,2,1,0:T(8,128)}, u32[]{:S(2)}, u32[]{:S(2)}) %collective-permute-start) | collective-permute-done | bytes 524320 | tf_op jit(solution)/shard_map/while/body/eval_jaxpr/ppermute | solution.py:13
  135.1 8.9 %collective-permute-done = f32[1,32,32,128]{3,2,1,0:T(8,128)} collective-permute-done((f32[1,32,32,128]{3,2,1,0:T(8,128)}, f32[1,32,32,128]{3,2,1,0:T(8,128)}, u32[]{:S(2)}, u32[]{:S(2)}) %collective-permute-start) | collective-permute-done | bytes 524320 | tf_op jit(solution)/shard_map/while/body/eval_jaxpr/ppermute | solution.py:13
  146.9 8.9 %collective-permute-done = f32[1,32,32,128]{3,2,1,0:T(8,128)} collective-permute-done((f32[1,32,32,128]{3,2,1,0:T(8,128)}, f32[1,32,32,128]{3,2,1,0:T(8,128)}, u32[]{:S(2)}, u32[]{:S(2)}) %collective-permute-start) | collective-permute-done | bytes 524320 | tf_op jit(solution)/shard_map/while/body/eval_jaxpr/ppermute | solution.py:13
  158.7 8.9 %collective-permute-done = f32[1,32,32,128]{3,2,1,0:T(8,128)} collective-permute-done((f32[1,32,32,128]{3,2,1,0:T(8,128)}, f32[1,32,32,128]{3,2,1,0:T(8,128)}, u32[]{:S(2)}, u32[]{:S(2)}) %collective-permute-start) | collective-permute-done | bytes 524320 | tf_op jit(solution)/shard_map/while/body/eval_jaxpr/ppermute | solution.py:13
  170.6 8.9 %collective-permute-done = f32[1,32,32,128]{3,2,1,0:T(8,128)} collective-permute-done((f32[1,32,32,128]{3,2,1,0:T(8,128)}, f32[1,32,32,128]{3,2,1,0:T(8,128)}, u32[]{:S(2)}, u32[]{:S(2)}) %collective-permute-start) | collective-permute-done | bytes 524320 | tf_op jit(solution)/shard_map/while/body/eval_jaxpr/ppermute | solution.py:13
  182.4 8.9 %collective-permute-done = f32[1,32,32,128]{3,2,1,0:T(8,128)} collective-permute-done((f32[1,32,32,128]{3,2,1,0:T(8,128)}, f32[1,32,32,128]{3,2,1,0:T(8,128)}, u32[]{:S(2)}, u32[]{:S(2)}) %collective-permute-start) | collective-permute-done | bytes 524320 | tf_op jit(solution)/shard_map/while/body/eval_jaxpr/ppermute | solution.py:13
  194.2 8.9 %collective-permute-done = f32[1,32,32,128]{3,2,1,0:T(8,128)} collective-permute-done((f32[1,32,32,128]{3,2,1,0:T(8,128)}, f32[1,32,32,128]{3,2,1,0:T(8,128)}, u32[]{:S(2)}, u32[]{:S(2)}) %collective-permute-start) | collective-permute-done | bytes 524320 | tf_op jit(solution)/shard_map/while/body/eval_jaxpr/ppermute | solution.py:13
  225.6 167.3 %while.31 = (s32[]{:T(128)}, f32[1,32,32,128]{3,2,1,0:T(8,128)S(1)}, s32[]{:T(128)}, f32[1,32,32,128]{3,2,1,0:T(8,128)S(1)}, f32[1,32,32,128]{3,2,1,0:T(8,128)S(...) while((s32[]{:T(128)}, ...), condition=%wide.region_7.8_spmd, body=%wide.region_4.7_spmd.sunk | while | flops 304087040 | bytes 23626028 | solution.py:136
  228.5 4.2 collective-permute-done.1
  233.6 3.7 collective-permute-start.1
  237.3 4.2 collective-permute-done.1
  242.4 3.7 collective-permute-start.1
  246.1 4.2 collective-permute-done.1
  251.2 3.7 collective-permute-start.1
  255.0 5.3 collective-permute-done.1
  261.2 2.6 collective-permute-start.1
  263.8 8.7 %collective-permute-done.1 = bf16[1,32,32,128]{3,2,1,0:T(8,128)(2,1)S(1)} collective-permute-done((bf16[1,32,32,128]{3,2,1,0:T(8,128)(2,1)}, bf16[1,32,32,128]{3,2,1,0:T(8,128)(2,1)S(1)}, u32[]{:S(2)}, u32[]{:S(2)}) %collective-permute-start.1) | collective-permute-done | bytes 262176 | tf_op jit(solution)/shard_map/while/body/eval_jaxpr/ppermute | solution.py:13
  275.4 7.9 %collective-permute-done.1 = bf16[1,32,32,128]{3,2,1,0:T(8,128)(2,1)S(1)} collective-permute-done((bf16[1,32,32,128]{3,2,1,0:T(8,128)(2,1)}, bf16[1,32,32,128]{3,2,1,0:T(8,128)(2,1)S(1)}, u32[]{:S(2)}, u32[]{:S(2)}) %collective-permute-start.1) | collective-permute-done | bytes 262176 | tf_op jit(solution)/shard_map/while/body/eval_jaxpr/ppermute | solution.py:13
  286.2 7.2 %collective-permute-done.1 = bf16[1,32,32,128]{3,2,1,0:T(8,128)(2,1)S(1)} collective-permute-done((bf16[1,32,32,128]{3,2,1,0:T(8,128)(2,1)}, bf16[1,32,32,128]{3,2,1,0:T(8,128)(2,1)S(1)}, u32[]{:S(2)}, u32[]{:S(2)}) %collective-permute-start.1) | collective-permute-done | bytes 262176 | tf_op jit(solution)/shard_map/while/body/eval_jaxpr/ppermute | solution.py:13
  296.2 7.2 %collective-permute-done.1 = bf16[1,32,32,128]{3,2,1,0:T(8,128)(2,1)S(1)} collective-permute-done((bf16[1,32,32,128]{3,2,1,0:T(8,128)(2,1)}, bf16[1,32,32,128]{3,2,1,0:T(8,128)(2,1)S(1)}, u32[]{:S(2)}, u32[]{:S(2)}) %collective-permute-start.1) | collective-permute-done | bytes 262176 | tf_op jit(solution)/shard_map/while/body/eval_jaxpr/ppermute | solution.py:13
  306.2 7.2 %collective-permute-done.1 = bf16[1,32,32,128]{3,2,1,0:T(8,128)(2,1)S(1)} collective-permute-done((bf16[1,32,32,128]{3,2,1,0:T(8,128)(2,1)}, bf16[1,32,32,128]{3,2,1,0:T(8,128)(2,1)S(1)}, u32[]{:S(2)}, u32[]{:S(2)}) %collective-permute-start.1) | collective-permute-done | bytes 262176 | tf_op jit(solution)/shard_map/while/body/eval_jaxpr/ppermute | solution.py:13
  316.3 7.2 %collective-permute-done.1 = bf16[1,32,32,128]{3,2,1,0:T(8,128)(2,1)S(1)} collective-permute-done((bf16[1,32,32,128]{3,2,1,0:T(8,128)(2,1)}, bf16[1,32,32,128]{3,2,1,0:T(8,128)(2,1)S(1)}, u32[]{:S(2)}, u32[]{:S(2)}) %collective-permute-start.1) | collective-permute-done | bytes 262176 | tf_op jit(solution)/shard_map/while/body/eval_jaxpr/ppermute | solution.py:13
  326.3 7.2 %collective-permute-done.1 = bf16[1,32,32,128]{3,2,1,0:T(8,128)(2,1)S(1)} collective-permute-done((bf16[1,32,32,128]{3,2,1,0:T(8,128)(2,1)}, bf16[1,32,32,128]{3,2,1,0:T(8,128)(2,1)S(1)}, u32[]{:S(2)}, u32[]{:S(2)}) %collective-permute-start.1) | collective-permute-done | bytes 262176 | tf_op jit(solution)/shard_map/while/body/eval_jaxpr/ppermute | solution.py:13
  336.4 7.2 %collective-permute-done.1 = bf16[1,32,32,128]{3,2,1,0:T(8,128)(2,1)S(1)} collective-permute-done((bf16[1,32,32,128]{3,2,1,0:T(8,128)(2,1)}, bf16[1,32,32,128]{3,2,1,0:T(8,128)(2,1)S(1)}, u32[]{:S(2)}, u32[]{:S(2)}) %collective-permute-start.1) | collective-permute-done | bytes 262176 | tf_op jit(solution)/shard_map/while/body/eval_jaxpr/ppermute | solution.py:13
  346.4 23.9 %collective-permute-done.1 = bf16[1,32,32,128]{3,2,1,0:T(8,128)(2,1)S(1)} collective-permute-done((bf16[1,32,32,128]{3,2,1,0:T(8,128)(2,1)}, bf16[1,32,32,128]{3,2,1,0:T(8,128)(2,1)S(1)}, u32[]{:S(2)}, u32[]{:S(2)}) %collective-permute-start.1) | collective-permute-done | bytes 262176 | tf_op jit(solution)/shard_map/while/body/eval_jaxpr/ppermute | solution.py:13
  370.4 3.3 conditional.5
  376.4 4.2 collective-permute-done.1
  381.5 7.0 %collective-permute-start.1 = (bf16[1,32,32,128]{3,2,1,0:T(8,128)(2,1)}, bf16[1,32,32,128]{3,2,1,0:T(8,128)(2,1)S(1)}, u32[]{:S(2)}, u32[]{:S(2)}) collective-permute-start(bf16[1,32,32,128]{3,2,1,0:T(8,128)(2,1)} %copy-done.10), channel_id=1, source_target_pairs={{16,0},{32,16},{48,32},{64,48},{80,64},{96,80},{112,96},{128,112},... | collective-permute-start | bytes 786440 | tf_op jit(solution)/shard_map/while/body/eval_jaxpr/ppermute | solution.py:13
  388.5 4.2 collective-permute-done.1
  417.7 41.7 %psum.7 = bf16[4,128]{1,0:T(4,128)(2,1)S(1)} all-reduce(bf16[4,128]{1,0:T(4,128)(2,1)S(1)} %pad_maximum_fusion.1), channel_id=1, replica_groups=mesh['layer'=16,'dp'=16] {'dp'}, use_global_device_ids=true, to_apply=%region_13.14 | all-reduce | flops 512 | bytes 2048 | tf_op jit(solution)/shard_map/psum | solution.py:152
  463.9 85.0 %all-gather.2.cloned.1.call-done = bf16[16,4,9,128,128]{4,3,2,1,0:T(8,128)(2,1)} async-done(((bf16[1,4,9,128,128]{4,3,2,1,0:T(8,128)(2,1)}), bf16[16,4,9,128,128]{4,3,2,1,0:T(8,128)(2,1)}) %all-gather.2.cloned.1.call-update) | async-done | bytes 18874384 | tf_op jit(solution)/shard_map/all_gather | solution.py:149
  548.8 10.6 %reduce_sum.48 = bf16[4,9,128,128]{3,2,1,0:T(8,128)(2,1)S(1)} reduce(bf16[16,4,9,128,128]{4,3,2,1,0:T(8,128)(2,1)} %all-gather.2.cloned.1.call-done, bf16[]{:T(256)} %constant.73.clone.1), dimensions={0}, to_apply=%region_8.9 | reduce | flops 8847360 | bytes 20054018 | tf_op jit(solution)/shard_map/reduce_sum | solution.py:149
  (430 shorter events, 148.7 us)
Async XLA Ops:
  7.2 2.1 copy-start
  7.2 2.1 copy-start.1
  7.2 541.7 %all-gather.2.cloned.1.call-start = ((), (), s32[]{:S(2)}) async-start(), calls=%async_computation | async-start | bytes 20054016 | tf_op jit(solution)/shard_map/all_gather | solution.py:149
  21.0 10.8 %collective-permute-start = (f32[1,32,32,128]{3,2,1,0:T(8,128)}, f32[1,32,32,128]{3,2,1,0:T(8,128)}, u32[]{:S(2)}, u32[]{:S(2)}) collective-permute-start(f32[1,32,32,128]{3,2,1,0:T(8,128)} %get-tuple-element.735), channel_id=1, source_target_pairs={{0,16},{16,32},{32,48},{48,64},{64,80},{80,96},{96,112},{112,128},... | collective-permute-start | bytes 1572872 | tf_op jit(solution)/shard_map/while/body/eval_jaxpr/ppermute | solution.py:13
  32.8 12.4 %collective-permute-start = (f32[1,32,32,128]{3,2,1,0:T(8,128)}, f32[1,32,32,128]{3,2,1,0:T(8,128)}, u32[]{:S(2)}, u32[]{:S(2)}) collective-permute-start(f32[1,32,32,128]{3,2,1,0:T(8,128)} %get-tuple-element.735), channel_id=1, source_target_pairs={{0,16},{16,32},{32,48},{48,64},{64,80},{80,96},{96,112},{112,128},... | collective-permute-start | bytes 1572872 | tf_op jit(solution)/shard_map/while/body/eval_jaxpr/ppermute | solution.py:13
  48.3 1.0 copy-start.3
  50.3 10.8 %collective-permute-start = (f32[1,32,32,128]{3,2,1,0:T(8,128)}, f32[1,32,32,128]{3,2,1,0:T(8,128)}, u32[]{:S(2)}, u32[]{:S(2)}) collective-permute-start(f32[1,32,32,128]{3,2,1,0:T(8,128)} %get-tuple-element.735), channel_id=1, source_target_pairs={{0,16},{16,32},{32,48},{48,64},{64,80},{80,96},{96,112},{112,128},... | collective-permute-start | bytes 1572872 | tf_op jit(solution)/shard_map/while/body/eval_jaxpr/ppermute | solution.py:13
  62.2 10.8 %collective-permute-start = (f32[1,32,32,128]{3,2,1,0:T(8,128)}, f32[1,32,32,128]{3,2,1,0:T(8,128)}, u32[]{:S(2)}, u32[]{:S(2)}) collective-permute-start(f32[1,32,32,128]{3,2,1,0:T(8,128)} %get-tuple-element.735), channel_id=1, source_target_pairs={{0,16},{16,32},{32,48},{48,64},{64,80},{80,96},{96,112},{112,128},... | collective-permute-start | bytes 1572872 | tf_op jit(solution)/shard_map/while/body/eval_jaxpr/ppermute | solution.py:13
  74.0 10.8 %collective-permute-start = (f32[1,32,32,128]{3,2,1,0:T(8,128)}, f32[1,32,32,128]{3,2,1,0:T(8,128)}, u32[]{:S(2)}, u32[]{:S(2)}) collective-permute-start(f32[1,32,32,128]{3,2,1,0:T(8,128)} %get-tuple-element.735), channel_id=1, source_target_pairs={{0,16},{16,32},{32,48},{48,64},{64,80},{80,96},{96,112},{112,128},... | collective-permute-start | bytes 1572872 | tf_op jit(solution)/shard_map/while/body/eval_jaxpr/ppermute | solution.py:13
  85.8 10.8 %collective-permute-start = (f32[1,32,32,128]{3,2,1,0:T(8,128)}, f32[1,32,32,128]{3,2,1,0:T(8,128)}, u32[]{:S(2)}, u32[]{:S(2)}) collective-permute-start(f32[1,32,32,128]{3,2,1,0:T(8,128)} %get-tuple-element.735), channel_id=1, source_target_pairs={{0,16},{16,32},{32,48},{48,64},{64,80},{80,96},{96,112},{112,128},... | collective-permute-start | bytes 1572872 | tf_op jit(solution)/shard_map/while/body/eval_jaxpr/ppermute | solution.py:13
  97.7 10.8 %collective-permute-start = (f32[1,32,32,128]{3,2,1,0:T(8,128)}, f32[1,32,32,128]{3,2,1,0:T(8,128)}, u32[]{:S(2)}, u32[]{:S(2)}) collective-permute-start(f32[1,32,32,128]{3,2,1,0:T(8,128)} %get-tuple-element.735), channel_id=1, source_target_pairs={{0,16},{16,32},{32,48},{48,64},{64,80},{80,96},{96,112},{112,128},... | collective-permute-start | bytes 1572872 | tf_op jit(solution)/shard_map/while/body/eval_jaxpr/ppermute | solution.py:13
  109.5 10.8 %collective-permute-start = (f32[1,32,32,128]{3,2,1,0:T(8,128)}, f32[1,32,32,128]{3,2,1,0:T(8,128)}, u32[]{:S(2)}, u32[]{:S(2)}) collective-permute-start(f32[1,32,32,128]{3,2,1,0:T(8,128)} %get-tuple-element.735), channel_id=1, source_target_pairs={{0,16},{16,32},{32,48},{48,64},{64,80},{80,96},{96,112},{112,128},... | collective-permute-start | bytes 1572872 | tf_op jit(solution)/shard_map/while/body/eval_jaxpr/ppermute | solution.py:13
  121.3 10.8 %collective-permute-start = (f32[1,32,32,128]{3,2,1,0:T(8,128)}, f32[1,32,32,128]{3,2,1,0:T(8,128)}, u32[]{:S(2)}, u32[]{:S(2)}) collective-permute-start(f32[1,32,32,128]{3,2,1,0:T(8,128)} %get-tuple-element.735), channel_id=1, source_target_pairs={{0,16},{16,32},{32,48},{48,64},{64,80},{80,96},{96,112},{112,128},... | collective-permute-start | bytes 1572872 | tf_op jit(solution)/shard_map/while/body/eval_jaxpr/ppermute | solution.py:13
  133.2 10.8 %collective-permute-start = (f32[1,32,32,128]{3,2,1,0:T(8,128)}, f32[1,32,32,128]{3,2,1,0:T(8,128)}, u32[]{:S(2)}, u32[]{:S(2)}) collective-permute-start(f32[1,32,32,128]{3,2,1,0:T(8,128)} %get-tuple-element.735), channel_id=1, source_target_pairs={{0,16},{16,32},{32,48},{48,64},{64,80},{80,96},{96,112},{112,128},... | collective-permute-start | bytes 1572872 | tf_op jit(solution)/shard_map/while/body/eval_jaxpr/ppermute | solution.py:13
  145.0 10.8 %collective-permute-start = (f32[1,32,32,128]{3,2,1,0:T(8,128)}, f32[1,32,32,128]{3,2,1,0:T(8,128)}, u32[]{:S(2)}, u32[]{:S(2)}) collective-permute-start(f32[1,32,32,128]{3,2,1,0:T(8,128)} %get-tuple-element.735), channel_id=1, source_target_pairs={{0,16},{16,32},{32,48},{48,64},{64,80},{80,96},{96,112},{112,128},... | collective-permute-start | bytes 1572872 | tf_op jit(solution)/shard_map/while/body/eval_jaxpr/ppermute | solution.py:13
  156.8 10.8 %collective-permute-start = (f32[1,32,32,128]{3,2,1,0:T(8,128)}, f32[1,32,32,128]{3,2,1,0:T(8,128)}, u32[]{:S(2)}, u32[]{:S(2)}) collective-permute-start(f32[1,32,32,128]{3,2,1,0:T(8,128)} %get-tuple-element.735), channel_id=1, source_target_pairs={{0,16},{16,32},{32,48},{48,64},{64,80},{80,96},{96,112},{112,128},... | collective-permute-start | bytes 1572872 | tf_op jit(solution)/shard_map/while/body/eval_jaxpr/ppermute | solution.py:13
  168.6 10.8 %collective-permute-start = (f32[1,32,32,128]{3,2,1,0:T(8,128)}, f32[1,32,32,128]{3,2,1,0:T(8,128)}, u32[]{:S(2)}, u32[]{:S(2)}) collective-permute-start(f32[1,32,32,128]{3,2,1,0:T(8,128)} %get-tuple-element.735), channel_id=1, source_target_pairs={{0,16},{16,32},{32,48},{48,64},{64,80},{80,96},{96,112},{112,128},... | collective-permute-start | bytes 1572872 | tf_op jit(solution)/shard_map/while/body/eval_jaxpr/ppermute | solution.py:13
  180.5 10.8 %collective-permute-start = (f32[1,32,32,128]{3,2,1,0:T(8,128)}, f32[1,32,32,128]{3,2,1,0:T(8,128)}, u32[]{:S(2)}, u32[]{:S(2)}) collective-permute-start(f32[1,32,32,128]{3,2,1,0:T(8,128)} %get-tuple-element.735), channel_id=1, source_target_pairs={{0,16},{16,32},{32,48},{48,64},{64,80},{80,96},{96,112},{112,128},... | collective-permute-start | bytes 1572872 | tf_op jit(solution)/shard_map/while/body/eval_jaxpr/ppermute | solution.py:13
  192.3 10.8 %collective-permute-start = (f32[1,32,32,128]{3,2,1,0:T(8,128)}, f32[1,32,32,128]{3,2,1,0:T(8,128)}, u32[]{:S(2)}, u32[]{:S(2)}) collective-permute-start(f32[1,32,32,128]{3,2,1,0:T(8,128)} %get-tuple-element.735), channel_id=1, source_target_pairs={{0,16},{16,32},{32,48},{48,64},{64,80},{80,96},{96,112},{112,128},... | collective-permute-start | bytes 1572872 | tf_op jit(solution)/shard_map/while/body/eval_jaxpr/ppermute | solution.py:13
  203.5 1.2 copy-start.13
  205.9 1.2 copy-start.15
  208.2 12.5 %copy-start.6 = (f32[1024,128]{1,0:T(8,128)}, f32[1024,128]{1,0:T(8,128)S(1)}, u32[]{:S(2)}) copy-start(f32[1024,128]{1,0:T(8,128)S(1)} %convolution_add_fusion.96) | copy-start | bytes 1572868
  208.4 1.2 copy-start.17
  208.4 2.3 copy-start.11
  210.7 7.3 %copy-start.4 = (f32[1024,128]{1,0:T(8,128)}, f32[1024,128]{1,0:T(8,128)S(1)}, u32[]{:S(2)}) copy-start(f32[1024,128]{1,0:T(8,128)S(1)} %convolution_add_fusion.88) | copy-start | bytes 1572868
  210.8 1.2 copy-start.19
  226.6 6.1 %collective-permute-start.1 = (bf16[1,32,32,128]{3,2,1,0:T(8,128)(2,1)}, bf16[1,32,32,128]{3,2,1,0:T(8,128)(2,1)S(1)}, u32[]{:S(2)}, u32[]{:S(2)}) collective-permute-start(bf16[1,32,32,128]{3,2,1,0:T(8,128)(2,1)} %copy-done.10), channel_id=1, source_target_pairs={{16,0},{32,16},{48,32},{64,48},{80,64},{96,80},{112,96},{128,112},... | collective-permute-start | bytes 786440 | tf_op jit(solution)/shard_map/while/body/eval_jaxpr/ppermute | solution.py:13
  233.6 7.9 %collective-permute-start.1 = (bf16[1,32,32,128]{3,2,1,0:T(8,128)(2,1)}, bf16[1,32,32,128]{3,2,1,0:T(8,128)(2,1)S(1)}, u32[]{:S(2)}, u32[]{:S(2)}) collective-permute-start(bf16[1,32,32,128]{3,2,1,0:T(8,128)(2,1)} %copy-done.10), channel_id=1, source_target_pairs={{16,0},{32,16},{48,32},{64,48},{80,64},{96,80},{112,96},{128,112},... | collective-permute-start | bytes 786440 | tf_op jit(solution)/shard_map/while/body/eval_jaxpr/ppermute | solution.py:13
  242.4 7.9 %collective-permute-start.1 = (bf16[1,32,32,128]{3,2,1,0:T(8,128)(2,1)}, bf16[1,32,32,128]{3,2,1,0:T(8,128)(2,1)S(1)}, u32[]{:S(2)}, u32[]{:S(2)}) collective-permute-start(bf16[1,32,32,128]{3,2,1,0:T(8,128)(2,1)} %copy-done.10), channel_id=1, source_target_pairs={{16,0},{32,16},{48,32},{64,48},{80,64},{96,80},{112,96},{128,112},... | collective-permute-start | bytes 786440 | tf_op jit(solution)/shard_map/while/body/eval_jaxpr/ppermute | solution.py:13
  251.2 9.0 %collective-permute-start.1 = (bf16[1,32,32,128]{3,2,1,0:T(8,128)(2,1)}, bf16[1,32,32,128]{3,2,1,0:T(8,128)(2,1)S(1)}, u32[]{:S(2)}, u32[]{:S(2)}) collective-permute-start(bf16[1,32,32,128]{3,2,1,0:T(8,128)(2,1)} %copy-done.10), channel_id=1, source_target_pairs={{16,0},{32,16},{48,32},{64,48},{80,64},{96,80},{112,96},{128,112},... | collective-permute-start | bytes 786440 | tf_op jit(solution)/shard_map/while/body/eval_jaxpr/ppermute | solution.py:13
  261.2 11.4 %collective-permute-start.1 = (bf16[1,32,32,128]{3,2,1,0:T(8,128)(2,1)}, bf16[1,32,32,128]{3,2,1,0:T(8,128)(2,1)S(1)}, u32[]{:S(2)}, u32[]{:S(2)}) collective-permute-start(bf16[1,32,32,128]{3,2,1,0:T(8,128)(2,1)} %copy-done.10), channel_id=1, source_target_pairs={{16,0},{32,16},{48,32},{64,48},{80,64},{96,80},{112,96},{128,112},... | collective-permute-start | bytes 786440 | tf_op jit(solution)/shard_map/while/body/eval_jaxpr/ppermute | solution.py:13
  273.5 9.8 %collective-permute-start.1 = (bf16[1,32,32,128]{3,2,1,0:T(8,128)(2,1)}, bf16[1,32,32,128]{3,2,1,0:T(8,128)(2,1)S(1)}, u32[]{:S(2)}, u32[]{:S(2)}) collective-permute-start(bf16[1,32,32,128]{3,2,1,0:T(8,128)(2,1)} %copy-done.10), channel_id=1, source_target_pairs={{16,0},{32,16},{48,32},{64,48},{80,64},{96,80},{112,96},{128,112},... | collective-permute-start | bytes 786440 | tf_op jit(solution)/shard_map/while/body/eval_jaxpr/ppermute | solution.py:13
  284.2 9.1 %collective-permute-start.1 = (bf16[1,32,32,128]{3,2,1,0:T(8,128)(2,1)}, bf16[1,32,32,128]{3,2,1,0:T(8,128)(2,1)S(1)}, u32[]{:S(2)}, u32[]{:S(2)}) collective-permute-start(bf16[1,32,32,128]{3,2,1,0:T(8,128)(2,1)} %copy-done.10), channel_id=1, source_target_pairs={{16,0},{32,16},{48,32},{64,48},{80,64},{96,80},{112,96},{128,112},... | collective-permute-start | bytes 786440 | tf_op jit(solution)/shard_map/while/body/eval_jaxpr/ppermute | solution.py:13
  294.3 9.1 %collective-permute-start.1 = (bf16[1,32,32,128]{3,2,1,0:T(8,128)(2,1)}, bf16[1,32,32,128]{3,2,1,0:T(8,128)(2,1)S(1)}, u32[]{:S(2)}, u32[]{:S(2)}) collective-permute-start(bf16[1,32,32,128]{3,2,1,0:T(8,128)(2,1)} %copy-done.10), channel_id=1, source_target_pairs={{16,0},{32,16},{48,32},{64,48},{80,64},{96,80},{112,96},{128,112},... | collective-permute-start | bytes 786440 | tf_op jit(solution)/shard_map/while/body/eval_jaxpr/ppermute | solution.py:13
  304.3 9.1 %collective-permute-start.1 = (bf16[1,32,32,128]{3,2,1,0:T(8,128)(2,1)}, bf16[1,32,32,128]{3,2,1,0:T(8,128)(2,1)S(1)}, u32[]{:S(2)}, u32[]{:S(2)}) collective-permute-start(bf16[1,32,32,128]{3,2,1,0:T(8,128)(2,1)} %copy-done.10), channel_id=1, source_target_pairs={{16,0},{32,16},{48,32},{64,48},{80,64},{96,80},{112,96},{128,112},... | collective-permute-start | bytes 786440 | tf_op jit(solution)/shard_map/while/body/eval_jaxpr/ppermute | solution.py:13
  314.4 9.1 %collective-permute-start.1 = (bf16[1,32,32,128]{3,2,1,0:T(8,128)(2,1)}, bf16[1,32,32,128]{3,2,1,0:T(8,128)(2,1)S(1)}, u32[]{:S(2)}, u32[]{:S(2)}) collective-permute-start(bf16[1,32,32,128]{3,2,1,0:T(8,128)(2,1)} %copy-done.10), channel_id=1, source_target_pairs={{16,0},{32,16},{48,32},{64,48},{80,64},{96,80},{112,96},{128,112},... | collective-permute-start | bytes 786440 | tf_op jit(solution)/shard_map/while/body/eval_jaxpr/ppermute | solution.py:13
  324.4 9.1 %collective-permute-start.1 = (bf16[1,32,32,128]{3,2,1,0:T(8,128)(2,1)}, bf16[1,32,32,128]{3,2,1,0:T(8,128)(2,1)S(1)}, u32[]{:S(2)}, u32[]{:S(2)}) collective-permute-start(bf16[1,32,32,128]{3,2,1,0:T(8,128)(2,1)} %copy-done.10), channel_id=1, source_target_pairs={{16,0},{32,16},{48,32},{64,48},{80,64},{96,80},{112,96},{128,112},... | collective-permute-start | bytes 786440 | tf_op jit(solution)/shard_map/while/body/eval_jaxpr/ppermute | solution.py:13
  334.4 9.1 %collective-permute-start.1 = (bf16[1,32,32,128]{3,2,1,0:T(8,128)(2,1)}, bf16[1,32,32,128]{3,2,1,0:T(8,128)(2,1)S(1)}, u32[]{:S(2)}, u32[]{:S(2)}) collective-permute-start(bf16[1,32,32,128]{3,2,1,0:T(8,128)(2,1)} %copy-done.10), channel_id=1, source_target_pairs={{16,0},{32,16},{48,32},{64,48},{80,64},{96,80},{112,96},{128,112},... | collective-permute-start | bytes 786440 | tf_op jit(solution)/shard_map/while/body/eval_jaxpr/ppermute | solution.py:13
  344.5 25.8 %collective-permute-start.1 = (bf16[1,32,32,128]{3,2,1,0:T(8,128)(2,1)}, bf16[1,32,32,128]{3,2,1,0:T(8,128)(2,1)S(1)}, u32[]{:S(2)}, u32[]{:S(2)}) collective-permute-start(bf16[1,32,32,128]{3,2,1,0:T(8,128)(2,1)} %copy-done.10), channel_id=1, source_target_pairs={{16,0},{32,16},{48,32},{64,48},{80,64},{96,80},{112,96},{128,112},... | collective-permute-start | bytes 786440 | tf_op jit(solution)/shard_map/while/body/eval_jaxpr/ppermute | solution.py:13
  372.6 1.0 copy-start.2
  374.5 6.1 %collective-permute-start.1 = (bf16[1,32,32,128]{3,2,1,0:T(8,128)(2,1)}, bf16[1,32,32,128]{3,2,1,0:T(8,128)(2,1)S(1)}, u32[]{:S(2)}, u32[]{:S(2)}) collective-permute-start(bf16[1,32,32,128]{3,2,1,0:T(8,128)(2,1)} %copy-done.10), channel_id=1, source_target_pairs={{16,0},{32,16},{48,32},{64,48},{80,64},{96,80},{112,96},{128,112},... | collective-permute-start | bytes 786440 | tf_op jit(solution)/shard_map/while/body/eval_jaxpr/ppermute | solution.py:13
  381.5 11.2 %collective-permute-start.1 = (bf16[1,32,32,128]{3,2,1,0:T(8,128)(2,1)}, bf16[1,32,32,128]{3,2,1,0:T(8,128)(2,1)S(1)}, u32[]{:S(2)}, u32[]{:S(2)}) collective-permute-start(bf16[1,32,32,128]{3,2,1,0:T(8,128)(2,1)} %copy-done.10), channel_id=1, source_target_pairs={{16,0},{32,16},{48,32},{64,48},{80,64},{96,80},{112,96},{128,112},... | collective-permute-start | bytes 786440 | tf_op jit(solution)/shard_map/while/body/eval_jaxpr/ppermute | solution.py:13
  396.0 1.0 copy-start.5
  396.0 1.2 copy-start.9
  396.0 1.3 copy-start.12
  398.5 1.2 copy-start.20
  410.4 1.1 copy-start.14
  462.0 1.0 copy-start.21
  (19 other events, 14.6 us)
Sparse Core Ops, SparseCore 0:
  417.8 130.9 all-gather.1
